TPU v7x, 256 devices: a whole 4x4x8 slice. The times are simulated.
256 devices in a mesh: fsdp: 16 (over z_hi, x), tensor: 4 (over z_lo, core), replica: 4 (over y).
Axes of the slice: x: 4, y: 4, z: 8 (z_hi: 4, z_lo: 2; z = z_hi * 2 + z_lo), core: 2. Of those that a mesh axis runs over, the one named last changes fastest.
Arguments:
- activations: bfloat16 [24576, 8192], P(('fsdp', 'replica'))
- norm_gain: float32 [8192], replicated, may hold values from 0.1 to 1.9
- key_weight: bfloat16 [8192, 1024], P('fsdp', 'tensor'), may hold values from -0.0625 to 0.0625
- value_weight: bfloat16 [8192, 1024], P('fsdp', 'tensor'), may hold values from -0.0625 to 0.0625
- key_cot: bfloat16 [24576, 1024], P(('fsdp', 'replica'), 'tensor'), may hold values from -6 to 6
- value_cot: bfloat16 [24576, 1024], P(('fsdp', 'replica'), 'tensor'), may hold values from -6 to 6
- blocks: int32 [2, 64, 2], P(None, 'tensor'), may hold values from 0 to 127, as said below
Outputs:
- key_out: bfloat16 [24576, 1024], P(('fsdp', 'replica'), 'tensor')
- value_out: bfloat16 [24576, 1024], P(('fsdp', 'replica'), 'tensor')
- normed_grad: bfloat16 [24576, 8192], P(('fsdp', 'replica'), 'tensor')
- block_grads: float32 [2, 64, 4096], P(None, 'tensor')
Inputs may be any that keep to these rules, and one draw needn't show every extreme that they name: Each run of 16 entries of one projection names 16 distinct blocks of one tensor shard, as (row block below 128, column block below the shard's key columns / 64).
All inputs are finite; a program needn't handle non-finite values.
Results may differ from a plain program's by a relative error of at most 0.013.
Values may be sent and summed in bfloat16 or wider, within the bound.
A program may use at most 128 MiB of HBM per device.

v0:
```python
import jax
import jax.numpy as jnp
from jax import lax
from jax.sharding import PartitionSpec as P

D = 8192
BLK = 64


norm_epsilon = 1e-05


def local(activations, norm_gain, key_weight, value_weight, key_cot, value_cot, blocks):
    tok_rows = activations.shape[0]
    shard_width = key_weight.shape[1]
    widened = activations.astype(jnp.float32)
    inverse_rms = lax.rsqrt(jnp.mean(widened * widened, axis=1, keepdims=True) + norm_epsilon)
    normed = (widened * inverse_rms * norm_gain).astype(jnp.bfloat16)
    stacked = jnp.concatenate([key_weight, value_weight], axis=1)
    cot_both = jnp.concatenate([key_cot, value_cot], axis=1)
    contract_cols = (((1,), (1,)), ((), ()))
    shard_rows = lax.all_gather(stacked, "fsdp", axis=0, tiled=True)
    running = jnp.dot(normed, shard_rows, preferred_element_type=jnp.float32)
    whole = shard_rows
    running, whole = (running, whole)
    partial_value = lax.dot_general(
        cot_both, whole, contract_cols, preferred_element_type=jnp.float32
    ).astype(jnp.bfloat16)
    key_out = running[:, :shard_width].astype(jnp.bfloat16)
    value_out = running[:, shard_width:].astype(jnp.bfloat16)
    normed_grad = (
        lax.psum_scatter(partial_value, "tensor", scatter_dimension=1, tiled=True)
        .astype(jnp.float32)
        .astype(jnp.bfloat16)
    )
    row_index = blocks[:, :, 0].reshape(-1)
    column_index = blocks[:, :, 1]
    left_blocks = jnp.take(normed.reshape(tok_rows, D // BLK, BLK), row_index, axis=1)
    key_blocks = jnp.take(
        key_cot.reshape(tok_rows, shard_width // BLK, BLK), column_index[0], axis=1
    )
    value_blocks = jnp.take(
        value_cot.reshape(tok_rows, shard_width // BLK, BLK), column_index[1], axis=1
    )
    right_blocks = jnp.concatenate([key_blocks, value_blocks], axis=1)
    local_grads = jnp.einsum(
        "tbi,tbj->bij", left_blocks, right_blocks, preferred_element_type=jnp.float32
    )
    local_grads = local_grads.reshape(2, blocks.shape[1], BLK * BLK)
    block_grads = lax.psum(local_grads, ("fsdp", "replica"))
    return (key_out, value_out, normed_grad, block_grads)


def solution(mesh):
    in_specs = (
        P(("fsdp", "replica"), None),
        P(),
        P("fsdp", "tensor"),
        P("fsdp", "tensor"),
        P(("fsdp", "replica"), "tensor"),
        P(("fsdp", "replica"), "tensor"),
        P(None, "tensor", None),
    )
    out_specs = (
        P(("fsdp", "replica"), "tensor"),
        P(("fsdp", "replica"), "tensor"),
        P(("fsdp", "replica"), "tensor"),
        P(None, "tensor", None),
    )
    return jax.shard_map(local, mesh=mesh, in_specs=in_specs, out_specs=out_specs, check_vma=False)
```

profile of v0, /device:TPU:8, one launch (start us, length us, event | category | flops | bytes accessed | tf_op | source)
XLA Modules:
  0.0 862.2 jit_solution(1816326400129489290)
XLA Ops:
  8.0 0.0 all-gather.2.cloned.1.call-start
  8.0 1.9 pad_maximum_fusion
  9.9 0.0 all-reduce.2.cloned.1.call-start
  10.0 1.1 copy.12
  11.1 1.1 copy.13
  12.2 8.7 %copy.11 = bf16[384,8192]{0,1:T(8,128)(2,1)} copy(bf16[384,8192]{1,0:T(8,128)(2,1)} %param.9) | data formatting | bytes 12582912 | tf_op args[0]
  20.9 0.1 reshape_squeeze.6
  21.0 0.1 reshape_squeeze.5
  21.1 0.7 gather_fusion.1
  21.8 0.7 gather_fusion.2
  22.6 4.2 fusion
  26.8 8.2 fusion.2
  35.0 3.8 gather_fusion
  38.8 0.2 select_bitcast_fusion
  39.0 0.8 fusion.3
  39.8 1.2 reshape.75
  41.0 0.0 all-reduce.2.cloned.1.call-update
  41.0 0.0 reduce-scatter.2.cloned.1.call-start
  41.0 77.6 %all-gather.2.cloned.1.call-done = bf16[8192,512]{1,0:T(8,128)(2,1)} async-done(((bf16[512,512]{1,0:T(8,128)(2,1)}), bf16[8192,512]{1,0:T(8,128)(2,1)}) %all-gather.2.cloned.1.call-update) | async-done | bytes 8388624 | tf_op jit(solution)/shard_map/all_gather | solution.py:22
  118.6 9.7 %convolution_convert_fusion = bf16[384,8192]{1,0:T(8,128)(2,1)} fusion(bf16[8192,512]{1,0:T(8,128)(2,1)} %all-gather.2.cloned.1.call-done, bf16[384,256]{1,0:T(8,128)(2,1)S(1)} %copy-done, bf16[384,256]{1,0:T(8,128)(2,1)} %param.13), kind=kOutput, calls=%fused_computation.8 | convolution fusion | flops 3225157632 | bytes 15073280 | tf_op jit(solution)/shard_map/dot_general | solution.py:26
  128.3 8.6 %convolution_convert_fusion.1 = bf16[384,512]{1,0:T(8,128)(2,1)S(1)} fusion(bf16[384,8192]{0,1:T(8,128)(2,1)} %fusion.2, bf16[8192,512]{1,0:T(8,128)(2,1)} %all-gather.2.cloned.1.call-done), kind=kOutput, calls=%fused_computation.16 | convolution fusion | flops 3221422080 | bytes 15073280 | tf_op jit(solution)/shard_map/dot_general | solution.py:23
  136.9 0.8 fusion.18
  137.7 715.1 %all-reduce.2.cloned.1.call-done = f32[2,16,4096]{2,1,0:T(8,128)} async-done(((f32[2,16,4096]{2,1,0:T(8,128)}), f32[2,16,4096]{2,1,0:T(8,128)}) %all-reduce.2.cloned.1.call-update) | async-done | bytes 524304 | tf_op jit(solution)/shard_map/psum | solution.py:50
  852.9 1.9 copy.15
  (17 shorter events, 0.1 us)
Async XLA Ops:
  8.0 110.6 %all-gather.2.cloned.1.call-start = ((), (), s32[]{:S(2)}) async-start(), calls=%async_computation.1 | async-start | bytes 8912896 | tf_op jit(solution)/shard_map/all_gather | solution.py:22
  9.9 842.9 %all-reduce.2.cloned.1.call-start = ((), (), s32[]{:S(2)}) async-start(), calls=%async_computation.3 | async-start | bytes 1048576 | tf_op jit(solution)/shard_map/psum | solution.py:50
  12.2 8.7 %copy-start.2 = (s32[2,16,2]{1,2,0:T(2,128)S(1)}, s32[2,16,2]{1,2,0:T(2,128)}, u32[]{:S(2)}) copy-start(s32[2,16,2]{1,2,0:T(2,128)} %param.15) | copy-start | bytes 772
  21.1 5.7 copy-start.1
  38.7 79.9 %copy-start = (bf16[384,256]{1,0:T(8,128)(2,1)S(1)}, bf16[384,256]{1,0:T(8,128)(2,1)}, u32[]{:S(2)}) copy-start(bf16[384,256]{1,0:T(8,128)(2,1)} %param.14) | copy-start | bytes 589828
  41.0 811.9 %reduce-scatter.2.cloned.1.call-start = ((), (), s32[]{:S(2)}) async-start(), calls=%async_computation.2 | async-start | bytes 7864320 | tf_op jit(solution)/shard_map/reduce_scatter | solution.py:32
Sparse Core Ops, SparseCore 0:
  11.8 106.7 all-gather.1
  128.4 76.1 reduce-scatter.1
Sparse Core Ops, SparseCore 1:
  41.1 811.7 all-reduce.1
where the time goes:
time: 863 us; the launch traced here: 862 us
  waiting for transfers between devices  793 us (92%)
  local copies, waits for them, and re-layouts  20.1 us (2%)
  matrix products  19.1 us (2%)
  between operations  15.6 us (2%)
  other arithmetic  14.5 us (2%)
    psum x1, waiting for transfers between devices, local(): block_grads = lax.psum(local_grads, ('fsdp', 'replica'))  715 us
    all_gather x1, waiting for transfers between devices, local(): shard_rows = lax.all_gather(stacked, 'fsdp', axis=0, tiled=True)  77.6 us
  transfers between devices with their start and end apart: 3, of which 2 were waited for; matrix products, arithmetic and copies ran while one was open for 6% of the time, Pallas kernels for 0%

commit v1 on v0

v1 whole, which is shorter than its diff:
```python
import functools

import jax
import jax.numpy as jnp
from jax import lax
from jax.experimental import pallas as pl
from jax.experimental.pallas import tpu as pltpu
from jax.sharding import PartitionSpec as P

D = 8192
TOK = 384
EPS = 1e-05
F32 = jnp.float32
BF16 = jnp.bfloat16
ROWS = 64
RA = 64

AXP, AXM, AXFP, AXFM, BYP, BYM, BYFP, BYFM, AYP, AYM, AYFP, AYFM, BXP, BXM, BXFP, BXFM = range(16)
OP0, OP1, OM0, OM1, OFP, OFM, ZP, ZM, ZFP, ZFM = range(10)


def body(
    act_hbm, gain_hbm, kw_hbm, vw_hbm, kc_hbm, vc_hbm, blocks,
    key_out, value_out, grad_out, bg_out,
    wbuf, act, normed, gain, cot, acc, pbuf, rbuf, qbuf,
    g32, s1, r1, p1, s2, r2, p2, s3, r3, tall,
    ld, xs, xr, os, orr, bs, br, ss, sr, qs, qr,
):
    f = lax.axis_index("fsdp")
    t = lax.axis_index("tensor")
    y = lax.axis_index("replica")
    zh, x = f // 4, f % 4
    zl = t // 2

    def m4(v):
        return lax.rem(v + 4, 4)

    def xdev(d):
        return {"fsdp": zh * 4 + m4(x + d)}

    def ydev(d):
        return {"replica": m4(y + d)}

    def zdev(d):
        return {"fsdp": m4(zh + d) * 4 + x}

    sib = {"tensor": t + 1 - 2 * (t % 2)}
    zpair = {"tensor": lax.rem(t + 2, 4)}

    loads = []

    def load(src, dst):
        c = pltpu.make_async_copy(src, dst, ld.at[len(loads)])
        c.start()
        loads.append(c)

    load(kw_hbm, wbuf.at[zh, x, :, :, pl.ds(0, 256)])
    load(vw_hbm, wbuf.at[zh, x, :, :, pl.ds(256, 256)])
    load(gain_hbm, gain)
    for i in range(4):
        load((kc_hbm, vc_hbm)[i // 2].at[:, pl.ds(i % 2 * 128, 128)], cot.at[i])
    for i in range(TOK // ROWS):
        load(act_hbm.at[pl.ds(i * ROWS, ROWS)], act.at[pl.ds(i * ROWS, ROWS)])

    barrier = pltpu.get_barrier_semaphore()
    peers = [xdev(1), xdev(-1), xdev(2), ydev(1), ydev(-1), ydev(2), zdev(1), zdev(-1), zdev(2), sib, zpair]
    for peer in peers:
        pl.semaphore_signal(barrier, inc=1, device_id=peer, device_id_type=pl.DeviceIdType.MESH)
    pl.semaphore_wait(barrier, len(peers))

    sent = []

    def rcopy(src, dst, a, b, dev):
        return pltpu.make_async_remote_copy(
            src_ref=src, dst_ref=dst, send_sem=a, recv_sem=b, device_id=dev,
            device_id_type=pl.DeviceIdType.MESH,
        )

    def piece(kind, zz, px, py):
        a, b = pl.ds(0, RA), pl.ds(RA, 128 - RA)
        if kind in (AXP, AXM):
            return wbuf.at[zz, px, py, a]
        if kind == AXFP:
            return wbuf.at[zz, m4(px - 1), py, pl.ds(0, RA // 2)]
        if kind == AXFM:
            return wbuf.at[zz, m4(px + 1), py, pl.ds(RA // 2, RA // 2)]
        if kind in (BYP, BYM):
            return wbuf.at[zz, px, py, b]
        if kind == BYFP:
            return wbuf.at[zz, px, m4(py - 1), pl.ds(RA, (128 - RA) // 2)]
        if kind == BYFM:
            return wbuf.at[zz, px, m4(py + 1), pl.ds(RA + (128 - RA) // 2, (128 - RA) // 2)]
        if kind in (AYP, AYM):
            return wbuf.at[zz, :, py, a]
        if kind == AYFP:
            return wbuf.at[zz, pl.ds(0, 2), m4(py - 1), a]
        if kind == AYFM:
            return wbuf.at[zz, pl.ds(2, 2), m4(py + 1), a]
        if kind in (BXP, BXM):
            return wbuf.at[zz, px, :, b]
        if kind == BXFP:
            return wbuf.at[zz, m4(px - 1), pl.ds(0, 2), b]
        return wbuf.at[zz, m4(px + 1), pl.ds(2, 2), b]

    along_x = (AXP, AXM, AXFP, AXFM, BXP, BXM, BXFP, BXFM)
    plus = (AXP, AXFP, BYP, BYFP, AYP, AYFP, BXP, BXFP)

    def xy(kind, zz, incoming):
        d = 1 if kind in plus else -1
        back = d if incoming else 0
        if kind in along_x:
            ref, dev = piece(kind, zz, m4(x - back), y), xdev(d)
        else:
            ref, dev = piece(kind, zz, x, m4(y - back)), ydev(d)
        return rcopy(ref, ref, xs.at[kind, zz], xr.at[kind, zz], dev)

    def send(zz, *kinds):
        for kind in kinds:
            c = xy(kind, zz, False)
            c.start()
            sent.append(c)

    def recv(zz, *kinds):
        for kind in kinds:
            xy(kind, zz, True).wait_recv()

    def own(kind, incoming):
        d = 1 if kind in (OP0, OP1, OFP, ZP, ZFP) else -1
        back = d if incoming else 0
        px, pz = m4(x - back), m4(zh - back)
        if kind in (OP0, OM0):
            ref = wbuf.at[zh, px, pl.ds(0, 2)]
        elif kind in (OP1, OM1):
            ref = wbuf.at[zh, px, pl.ds(2, 2)]
        elif kind == OFP:
            ref = wbuf.at[zh, m4(px - 1), pl.ds(0, 2)]
        elif kind == OFM:
            ref = wbuf.at[zh, m4(px + 1), pl.ds(2, 2)]
        elif kind in (ZP, ZM):
            ref = wbuf.at[pz, x, y]
        elif kind == ZFP:
            ref = wbuf.at[m4(pz - 1), x, y, pl.ds(0, 64)]
        else:
            ref = wbuf.at[m4(pz + 1), x, y, pl.ds(64, 64)]
        dev = zdev(d) if kind >= ZP else xdev(d)
        return rcopy(ref, ref, os.at[kind], orr.at[kind], dev)

    def osend(*kinds):
        for kind in kinds:
            c = own(kind, False)
            c.start()
            sent.append(c)

    def orecv(*kinds):
        for kind in kinds:
            own(kind, True).wait_recv()

    def norm_rows(i):
        loads[7 + i].wait()

        @pl.loop(0, ROWS // 16)
        def _(k):
            rows = pl.ds(pl.multiple_of(i * ROWS + k * 16, 16), 16)
            total = jnp.zeros((16, 128), F32)
            for j in range(D // 512):
                v = act[rows, pl.ds(j * 512, 512)].astype(F32)
                v = v * v
                total = total + ((v[:, 0:128] + v[:, 128:256]) + (v[:, 256:384] + v[:, 384:512]))
            inv = lax.rsqrt(jnp.sum(total, axis=1, keepdims=True) / D + EPS)
            for j in range(D // 128):
                cols = pl.ds(j * 128, 128)
                v = act[rows, cols].astype(F32)
                normed[j, rows] = (v * inv * gain[:, cols]).astype(BF16)

    def block_entry(p, n):
        row, column = blocks[p, n, 0], blocks[p, n, 1]
        row_odd, column_odd = lax.rem(row, 2), lax.rem(column, 2)
        left = normed[lax.div(row, 2)]
        right = cot[2 * p + lax.div(column, 2)]
        full = lax.dot_general(left, right, (((0,), (0,)), ((), ())), preferred_element_type=F32)
        low = row_odd.astype(F32)
        half = full[64:] * low + full[:64] * (1.0 - low)
        move = column_odd.astype(F32) if p == 0 else 1.0 - column_odd.astype(F32)
        return pltpu.roll(half, 64, 1) * move + half * (1.0 - move)

    lane = lax.broadcasted_iota(jnp.int32, (64, 128), 1)

    def block_products(lo, hi):
        @pl.loop(lo, hi)
        def _(n):
            value = jnp.where(lane < 64, block_entry(0, n), block_entry(1, n))
            g32[n // 4, n % 4] = value
            s1[n // 4, n % 4] = value.astype(BF16)

    def shard(zz, xx):
        w = wbuf[zz, xx].reshape(512, 512)
        tile = (zz * 4 + xx) * 4
        left = jnp.concatenate([normed[tile + j] for j in range(4)], axis=1)
        acc[...] += jnp.dot(left, w, preferred_element_type=F32)
        both = jnp.concatenate([cot[j] for j in range(4)], axis=1)
        part = lax.dot_general(both, w, (((1,), (1,)), ((), ())), preferred_element_type=F32)
        pbuf[zz, xx] = part.astype(BF16)
        odd = lax.rem(zz + t, 2) == 1

        @pl.when(odd)
        def _():
            sibcopy(zz, xx).start()

    def sibcopy(zz, xx):
        slot = (zz // 2 - zl) * (zz // 2 - zl)
        return rcopy(pbuf.at[zz, xx], rbuf.at[slot, xx], ss.at[slot * 4 + xx], sr.at[slot * 4 + xx], sib)

    def qcopy(zz, xx):
        return rcopy(pbuf.at[zz, xx], qbuf.at[xx], qs.at[xx], qr.at[xx], zpair)

    def rwait(slot, xx):
        rcopy(rbuf.at[slot, xx], rbuf.at[slot, xx], ss.at[slot * 4 + xx], sr.at[slot * 4 + xx], sib).wait_recv()

    away = lax.rem(t + 2, 4)

    def combine(zz, xx):
        @pl.when(zz == away)
        def _():
            rwait(1, xx)
            pbuf[zz, xx] = (pbuf[zz, xx].astype(F32) + rbuf[1, xx].astype(F32)).astype(BF16)
            qcopy(zz, xx).start()

    dist = (1, -1, 2)

    def bg_copy(stage, d, incoming):
        back = d if incoming else 0
        axis = (0, 1, 2, 2, 1, 0)[stage]
        me = (y, x, zh)[axis]
        dev = (ydev, xdev, zdev)[axis](d)
        sender = m4(me - back)
        target = m4(sender + d)
        if stage < 3:
            src, dst = (s1, s2, s3)[stage].at[target], (r1, r2, r3)[stage].at[sender]
        else:
            where = [y, x, zh]
            where[axis] = sender
            src = dst = tall.at[tuple(where[: axis + 1])]
        i = stage * 3 + dist.index(d)
        return rcopy(src, dst, bs.at[i], br.at[i], dev)

    def bg_send(stage):
        for d in dist:
            c = bg_copy(stage, d, False)
            c.start()
            sent.append(c)

    def bg_recv(stage):
        for d in dist:
            bg_copy(stage, d, True).wait_recv()

    def bg_sum(stage):
        bg_recv(stage)
        if stage == 0:
            total = g32[y]
            for d in dist:
                total = total + r1[m4(y - d)].astype(F32)
            p1[...] = total
            s2[...] = total.astype(BF16)
        elif stage == 1:
            total = p1[x]
            for d in dist:
                total = total + r2[m4(x - d)].astype(F32)
            total = total.reshape(4, 16, 128)
            p2[...] = total
            s3[...] = total.astype(BF16)
        else:
            total = p2[zh]
            for d in dist:
                total = total + r3[m4(zh - d)].astype(F32)
            tall[y, x, zh] = total.astype(BF16)
        bg_send(stage + 1)

    own_away = (zh // 2 - zl) * (zh // 2 - zl)
    other = zh + 1 - 2 * (zh % 2)
    first = own_away * other + (1 - own_away) * (2 - 2 * zl)
    second = own_away * (2 * zl) + (1 - own_away) * (3 - 2 * zl)
    third = own_away * (2 * zl + 1) + (1 - own_away) * other
    order = (first, second, third)

    def small(zz):
        send(zz, AXP, AXM, BYP, BYM)

    def small_forward(zz):
        recv(zz, AXP, BYP)
        send(zz, AXFP, BYFP)
        recv(zz, AXM, BYM)
        send(zz, AXFM, BYFM)

    def big(zz):
        recv(zz, AXFP, AXFM)
        send(zz, AYP, AYM)
        recv(zz, BYFP, BYFM)
        send(zz, BXP, BXM)

    def big_forward(zz):
        recv(zz, AYP, BXP)
        send(zz, AYFP, BXFP)
        recv(zz, AYM, BXM)
        send(zz, AYFM, BXFM)

    def big_end(zz):
        recv(zz, AYFP, AYFM, BXFP, BXFM)

    loads[0].wait()
    loads[1].wait()
    osend(ZP, ZM, OP0, OM1, OP1, OM0)
    acc[...] = jnp.zeros_like(acc)
    loads[2].wait()
    for i in range(TOK // ROWS):
        norm_rows(i)
    orecv(ZP, ZM)
    osend(ZFP, ZFM)
    small(m4(zh - 1))
    small(m4(zh + 1))
    for i in range(3, 7):
        loads[i].wait()
    orecv(OP0)
    osend(OFP)
    orecv(OM1)
    osend(OFM)
    orecv(ZFP, ZFM)
    small(m4(zh + 2))
    block_products(0, 16)
    bg_send(0)
    small_forward(first)
    small_forward(second)
    small_forward(third)
    shard(zh, x)
    big(first)
    combine(zh, x)
    orecv(OP1, OM0)
    bg_sum(0)
    shard(zh, m4(x + 1))
    big(second)
    shard(zh, m4(x - 1))
    combine(zh, m4(x + 1))
    bg_sum(1)
    big(third)
    orecv(OFP, OFM)
    shard(zh, m4(x + 2))
    combine(zh, m4(x - 1))
    bg_sum(2)
    combine(zh, m4(x + 2))
    for k, zz in enumerate(order):
        big_forward(zz)
        big_end(zz)
        if k == 0:
            bg_recv(3)
            bg_send(4)
        if k == 1:
            bg_recv(4)
            bg_send(5)
        for i in range(4):
            shard(zz, i)
            if i > 0:
                combine(zz, i - 1)
        combine(zz, 3)
    key_out[...] = acc[:, 0:256].astype(BF16)
    value_out[...] = acc[:, 256:512].astype(BF16)
    bg_recv(5)
    bg_out[...] = tall[...].astype(F32).reshape(16, 64, 128)
    for i in range(4):
        rwait(0, i)
        rcopy(qbuf.at[i], qbuf.at[i], qs.at[i], qr.at[i], zpair).wait_recv()
        total = pbuf[t, i].astype(F32) + rbuf[0, i].astype(F32) + qbuf[i].astype(F32)
        grad_out[:, pl.ds(i * 512, 512)] = total.astype(BF16)

    for c in sent:
        c.wait_send()
    for i in range(4):
        for slot in range(2):
            rcopy(pbuf.at[0, i], rbuf.at[slot, i], ss.at[slot * 4 + i], sr.at[slot * 4 + i], sib).wait_send()
        qcopy(away, i).wait_send()


def local(activations, norm_gain, key_weight, value_weight, key_cot, value_cot, blocks):
    any_spec = pl.BlockSpec(memory_space=pl.ANY)
    vmem_spec = pl.BlockSpec(memory_space=pltpu.VMEM)
    dma = pltpu.SemaphoreType.DMA
    key_out, value_out, grad, bg = pl.pallas_call(
        body,
        out_shape=(
            jax.ShapeDtypeStruct((TOK, 256), BF16),
            jax.ShapeDtypeStruct((TOK, 256), BF16),
            jax.ShapeDtypeStruct((TOK, 2048), BF16),
            jax.ShapeDtypeStruct((16, 64, 128), F32),
        ),
        in_specs=[any_spec] * 6 + [pl.BlockSpec(memory_space=pltpu.SMEM)],
        out_specs=(vmem_spec,) * 4,
        scratch_shapes=[
            pltpu.VMEM((4, 4, 4, 128, 512), BF16),
            pltpu.VMEM((TOK, D), BF16),
            pltpu.VMEM((D // 128, TOK, 128), BF16),
            pltpu.VMEM((1, D), F32),
            pltpu.VMEM((4, TOK, 128), BF16),
            pltpu.VMEM((TOK, 512), F32),
            pltpu.VMEM((4, 4, TOK, 512), BF16),
            pltpu.VMEM((2, 4, TOK, 512), BF16),
            pltpu.VMEM((4, TOK, 512), BF16),
            pltpu.VMEM((4, 4, 64, 128), F32),
            pltpu.VMEM((4, 4, 64, 128), BF16),
            pltpu.VMEM((4, 4, 64, 128), BF16),
            pltpu.VMEM((4, 64, 128), F32),
            pltpu.VMEM((4, 64, 128), BF16),
            pltpu.VMEM((4, 64, 128), BF16),
            pltpu.VMEM((4, 16, 128), F32),
            pltpu.VMEM((4, 16, 128), BF16),
            pltpu.VMEM((4, 16, 128), BF16),
            pltpu.VMEM((4, 4, 4, 16, 128), BF16),
            dma((7 + TOK // ROWS,)),
            dma((16, 4)),
            dma((16, 4)),
            dma((10,)),
            dma((10,)),
            dma((18,)),
            dma((18,)),
            dma((8,)),
            dma((8,)),
            dma((4,)),
            dma((4,)),
        ],
        compiler_params=pltpu.CompilerParams(
            collective_id=0, has_side_effects=True, vmem_limit_bytes=60 * 1024 * 1024
        ),
        name="kv_step",
    )(
        activations,
        norm_gain.reshape(1, D),
        key_weight.reshape(4, 128, 256),
        value_weight.reshape(4, 128, 256),
        key_cot,
        value_cot,
        blocks,
    )
    bg = bg.reshape(16, 64, 2, 64).transpose(2, 0, 1, 3).reshape(2, 16, 4096)
    return key_out, value_out, grad, bg


def solution(mesh):
    in_specs = (
        P(("fsdp", "replica"), None),
        P(),
        P("fsdp", "tensor"),
        P("fsdp", "tensor"),
        P(("fsdp", "replica"), "tensor"),
        P(("fsdp", "replica"), "tensor"),
        P(None, "tensor", None),
    )
    out_specs = (
        P(("fsdp", "replica"), "tensor"),
        P(("fsdp", "replica"), "tensor"),
        P(("fsdp", "replica"), "tensor"),
        P(None, "tensor", None),
    )
    return jax.shard_map(local, mesh=mesh, in_specs=in_specs, out_specs=out_specs, check_vma=False)
```

time: 863 us -> 108 us (0.13)
  the two profiles are of different devices: /device:TPU:8 before, /device:TPU:1 now
where the time goes in v1:
time: 108 us; the launch traced here: 107 us
  Pallas kernels  98.3 us (91%)
  local copies, waits for them, and re-layouts  8.39 us (8%)
    pallas_call x1, Pallas kernels, local(): pl.pallas_call(body, out_shape=(jax.ShapeDtypeStruct((TOK, 256), BF16), j...  98.3 us
    unnamed x8, local copies, waits for them, and re-layouts  5.46 us
    reshape x2, local copies, waits for them, and re-layouts, local(): bg = bg.reshape(16, 64, 2, 64).transpose(2, 0, 1, 3).reshape(2, 16, 4096)  2.81 us

profile of v1, /device:TPU:1, one launch (start us, length us, event | category | flops | bytes accessed | tf_op | source)
XLA Modules:
  0.0 107.4 jit_solution(7428715185618268841)
XLA Ops:
  0.6 1.4 %copy.11.blocks = s32[2,16,2]{2,1,0:T(8,128)} copy(s32[2,16,2]{1,2,0:T(2,128)} %param.13) | data formatting | bytes 512 | tf_op args[6]
  2.0 98.3 %kv_step.1 = (bf16[384,256]{1,0:T(8,128)(2,1)}, bf16[384,256]{1,0:T(8,128)(2,1)}, bf16[384,2048]{1,0:T(8,128)(2,1)}, f32[16,64,128]{2,1,0:T(8,128)}) custom-call(bf16[384,8192]{1,0:T(8,128)(2,1)} %act_hbm.1, f32[1,8192]{1,0:T(1,128)} %bitcast.9, bf16[4,128,256]{2,1,0:T(8,128)(2,1)} %bitcast.7, bf16[4,128,256]{2,1,0:T(8,128)(2,1)} %bitcast.8, ...), custom_call_target="tpu_custom_call" | custom-call | tf_op jit(solution)/shard_map/kv_step/pallas_call | solution.py:385
  100.4 1.7 %reshape.26 = f32[16,64,2,64]{3,2,1,0:T(2,128)S(1)} reshape(f32[16,64,128]{2,1,0:T(8,128)} %get-tuple-element.11) | data formatting | bytes 1048576 | tf_op jit(solution)/shard_map/reshape | solution.py:440
  102.0 0.0 copy-start.1
  102.0 0.0 copy-start
  102.0 0.1 copy.12
  102.2 1.2 %reshape.27 = f32[2,16,4096]{2,1,0:T(8,128)} reshape(f32[2,16,64,64]{3,2,1,0:T(8,128)S(1)} %copy.12) | data formatting | bytes 1048576 | tf_op jit(solution)/shard_map/reshape | solution.py:440
  103.3 0.0 copy-done.1
  103.3 0.7 copy.16
  104.0 0.0 copy-done
  104.0 0.7 copy.17
  104.7 2.7 %copy.18 = bf16[384,2048]{1,0:T(8,128)(2,1)} copy(bf16[384,2048]{1,0:T(8,128)(2,1)} %get-tuple-element.18) | data formatting | bytes 3145728
Async XLA Ops:
  102.0 1.3 %copy-start.1 = (bf16[384,256]{1,0:T(8,128)(2,1)S(1)}, bf16[384,256]{1,0:T(8,128)(2,1)}, u32[]{:S(2)}) copy-start(bf16[384,256]{1,0:T(8,128)(2,1)} %get-tuple-element.16) | copy-start | bytes 589828
  102.0 2.0 %copy-start = (bf16[384,256]{1,0:T(8,128)(2,1)S(1)}, bf16[384,256]{1,0:T(8,128)(2,1)}, u32[]{:S(2)}) copy-start(bf16[384,256]{1,0:T(8,128)(2,1)} %get-tuple-element.17) | copy-start | bytes 589828

commit v2 on v1

v2 whole, which is shorter than its diff:
```python
import functools

import jax
import jax.numpy as jnp
from jax import lax
from jax.experimental import pallas as pl
from jax.experimental.pallas import tpu as pltpu
from jax.sharding import PartitionSpec as P

D = 8192
TOK = 384
EPS = 1e-05
F32 = jnp.float32
BF16 = jnp.bfloat16
ROWS = 64

AXP, AXM, AXFP, AXFM, BYP, BYM, BYFP, BYFM, AYP, AYM, AYFP, AYFM, BXP, BXM, BXFP, BXFM = range(16)
ZAP, ZAM, ZBP, ZBM, ZFP, ZFM = range(6)


def body(
    act_hbm, gain_hbm, kw_hbm, vw_hbm, kc_hbm, vc_hbm, blocks,
    key_out, value_out, grad_out, bg_out,
    wa, wb, act, normed, gain, cot, acc, pbuf, rbuf, qbuf,
    g32, s1, r1, p1, s2, r2, p2, s3, r3, tall,
    ld, xs, xr, zs, zr, bs, br, ss, sr, qs, qr,
):
    f = lax.axis_index("fsdp")
    t = lax.axis_index("tensor")
    y = lax.axis_index("replica")
    zh, x = f // 4, f % 4
    zl = t // 2

    def m4(v):
        return lax.rem(v + 4, 4)

    def xdev(d):
        return {"fsdp": zh * 4 + m4(x + d)}

    def ydev(d):
        return {"replica": m4(y + d)}

    def zdev(d):
        return {"fsdp": m4(zh + d) * 4 + x}

    sib = {"tensor": t + 1 - 2 * (t % 2)}
    zpair = {"tensor": lax.rem(t + 2, 4)}

    loads = []

    def load(src, dst):
        c = pltpu.make_async_copy(src, dst, ld.at[len(loads)])
        c.start()
        loads.append(c)

    for i, w_hbm in enumerate((kw_hbm, vw_hbm)):
        load(w_hbm.at[y, 0], wa.at[zh, y, x, :, pl.ds(i * 256, 256)])
        load(w_hbm.at[y, 1], wb.at[zh, x, y, :, pl.ds(i * 256, 256)])
    load(gain_hbm, gain)
    for i in range(4):
        load((kc_hbm, vc_hbm)[i // 2].at[:, pl.ds(i % 2 * 128, 128)], cot.at[i])
    first_rows = len(loads)
    for i in range(TOK // ROWS):
        load(act_hbm.at[pl.ds(i * ROWS, ROWS)], act.at[pl.ds(i * ROWS, ROWS)])

    barrier = pltpu.get_barrier_semaphore()
    peers = [xdev(1), xdev(-1), xdev(2), ydev(1), ydev(-1), ydev(2), zdev(1), zdev(-1), zdev(2), sib, zpair]
    for peer in peers:
        pl.semaphore_signal(barrier, inc=1, device_id=peer, device_id_type=pl.DeviceIdType.MESH)
    pl.semaphore_wait(barrier, len(peers))

    sent = []

    def rcopy(src, dst, a, b, dev):
        return pltpu.make_async_remote_copy(
            src_ref=src, dst_ref=dst, send_sem=a, recv_sem=b, device_id=dev,
            device_id_type=pl.DeviceIdType.MESH,
        )

    def piece(kind, zz, px, py):
        if kind in (AXP, AXM):
            return wa.at[zz, py, px]
        if kind == AXFP:
            return wa.at[zz, py, m4(px - 1), pl.ds(0, 32)]
        if kind == AXFM:
            return wa.at[zz, py, m4(px + 1), pl.ds(32, 32)]
        if kind in (BYP, BYM):
            return wb.at[zz, px, py]
        if kind == BYFP:
            return wb.at[zz, px, m4(py - 1), pl.ds(0, 32)]
        if kind == BYFM:
            return wb.at[zz, px, m4(py + 1), pl.ds(32, 32)]
        if kind in (AYP, AYM):
            return wa.at[zz, py]
        if kind == AYFP:
            return wa.at[zz, m4(py - 1), pl.ds(0, 2)]
        if kind == AYFM:
            return wa.at[zz, m4(py + 1), pl.ds(2, 2)]
        if kind in (BXP, BXM):
            return wb.at[zz, px]
        if kind == BXFP:
            return wb.at[zz, m4(px - 1), pl.ds(0, 2)]
        return wb.at[zz, m4(px + 1), pl.ds(2, 2)]

    along_x = (AXP, AXM, AXFP, AXFM, BXP, BXM, BXFP, BXFM)
    plus = (AXP, AXFP, BYP, BYFP, AYP, AYFP, BXP, BXFP)

    def xy(kind, zz, incoming):
        d = 1 if kind in plus else -1
        back = d if incoming else 0
        if kind in along_x:
            ref, dev = piece(kind, zz, m4(x - back), y), xdev(d)
        else:
            ref, dev = piece(kind, zz, x, m4(y - back)), ydev(d)
        return rcopy(ref, ref, xs.at[kind, zz], xr.at[kind, zz], dev)

    def send(zz, *kinds):
        for kind in kinds:
            c = xy(kind, zz, False)
            c.start()
            sent.append(c)

    def recv(zz, *kinds):
        for kind in kinds:
            xy(kind, zz, True).wait_recv()

    def along_z(kind, incoming):
        d = 1 if kind in (ZAP, ZBP, ZFP) else -1
        pz = m4(zh - d) if incoming else zh
        if kind in (ZAP, ZAM):
            ref = wa.at[pz, y, x]
        elif kind in (ZBP, ZBM):
            ref = wb.at[pz, x, y]
        elif kind == ZFP:
            ref = wa.at[m4(pz - 1), y, x]
        else:
            ref = wb.at[m4(pz + 1), x, y]
        return rcopy(ref, ref, zs.at[kind], zr.at[kind], zdev(d))

    def zsend(*kinds):
        for kind in kinds:
            c = along_z(kind, False)
            c.start()
            sent.append(c)

    def zrecv(*kinds):
        for kind in kinds:
            along_z(kind, True).wait_recv()

    def lanes(rows):
        return lax.broadcasted_iota(jnp.int32, (rows, 128), 1) < 64

    def norm_rows(i):
        loads[first_rows + i].wait()
        low = lanes(16)

        @pl.loop(0, ROWS // 16)
        def _(k):
            rows = pl.ds(pl.multiple_of(i * ROWS + k * 16, 16), 16)
            total = jnp.zeros((16, 128), F32)
            for j in range(D // 512):
                v = act[rows, pl.ds(j * 512, 512)].astype(F32)
                v = v * v
                total = total + ((v[:, 0:128] + v[:, 128:256]) + (v[:, 256:384] + v[:, 384:512]))
            inv = lax.rsqrt(jnp.sum(total, axis=1, keepdims=True) / D + EPS)

            def tile(zz, xx, q):
                cols = pl.ds((zz * 16 + xx * 4 + q) * 128, 128)
                return act[rows, cols].astype(F32) * inv * gain[:, cols]

            for zz in range(4):
                for hx in range(2):
                    for hq in range(2):
                        ee, eo = tile(zz, 2 * hx, 2 * hq), tile(zz, 2 * hx, 2 * hq + 1)
                        oe, oo = tile(zz, 2 * hx + 1, 2 * hq), tile(zz, 2 * hx + 1, 2 * hq + 1)
                        ree, roe, roo = pltpu.roll(ee, 64, 1), pltpu.roll(oe, 64, 1), pltpu.roll(oo, 64, 1)
                        a0, b0 = (zz * 4 + 2 * hq) * 2 + hx, ((4 + zz) * 4 + 2 * hx) * 2 + hq
                        normed[a0, rows] = jnp.where(low, ee, roe).astype(BF16)
                        normed[a0 + 2, rows] = jnp.where(low, eo, roo).astype(BF16)
                        normed[b0, rows] = jnp.where(low, ree, eo).astype(BF16)
                        normed[b0 + 2, rows] = jnp.where(low, roe, oo).astype(BF16)

    def block_entry(p, n):
        row, column = blocks[p, 0, n], blocks[p, 1, n]
        zz, xx, q, odd = lax.div(row, 32), lax.rem(lax.div(row, 8), 4), lax.rem(lax.div(row, 2), 4), lax.rem(row, 2)
        in_a = zz * 8 + q * 2 + lax.div(xx, 2)
        in_b = 32 + zz * 8 + xx * 2 + lax.div(q, 2)
        left = normed[in_a * (1 - odd) + in_b * odd]
        half = lax.rem(xx, 2) * (1 - odd) + lax.rem(q, 2) * odd
        right = cot[2 * p + lax.div(column, 2)]
        full = lax.dot_general(left, right, (((0,), (0,)), ((), ())), preferred_element_type=F32)
        low = half.astype(F32)
        half = full[64:] * low + full[:64] * (1.0 - low)
        column_odd = lax.rem(column, 2).astype(F32)
        move = column_odd if p == 0 else 1.0 - column_odd
        return pltpu.roll(half, 64, 1) * move + half * (1.0 - move)

    def block_products(lo, hi):
        low = lanes(64)

        @pl.loop(lo, hi)
        def _(n):
            value = jnp.where(low, block_entry(0, n), block_entry(1, n))
            g32[n // 4, n % 4] = value
            s1[n // 4, n % 4] = value.astype(BF16)

    away = lax.rem(t + 2, 4)

    def sib_index(zz, ab, i):
        return (zz // 2 - zl) * (zz // 2 - zl) * 8 + ab * 4 + i

    def sibcopy(zz, ab, i):
        n = sib_index(zz, ab, i)
        return rcopy(pbuf.at[zz, ab, i], rbuf.at[n], ss.at[n], sr.at[n], sib)

    def qcopy(ab, i):
        return rcopy(pbuf.at[away, ab, i], qbuf.at[ab * 4 + i], qs.at[ab * 4 + i], qr.at[ab * 4 + i], zpair)

    def rwait(slot, ab, i):
        n = slot * 8 + ab * 4 + i
        rcopy(rbuf.at[n], rbuf.at[n], ss.at[n], sr.at[n], sib).wait_recv()

    def unit(zz, ab, i):
        w = (wa, wb)[ab][zz, i].reshape(256, 512)
        tile = ((ab * 4 + zz) * 4 + i) * 2
        left = jnp.concatenate([normed[tile], normed[tile + 1]], axis=1)
        acc[...] += jnp.dot(left, w, preferred_element_type=F32)
        both = jnp.concatenate([cot[j] for j in range(4)], axis=1)
        part = lax.dot_general(both, w, (((1,), (1,)), ((), ())), preferred_element_type=F32)
        pbuf[zz, ab, i] = part.astype(BF16)

        @pl.when(lax.rem(zz + t, 2) == 1)
        def _():
            sibcopy(zz, ab, i).start()

    def combine(zz, ab, i):
        @pl.when(zz == away)
        def _():
            rwait(1, ab, i)
            pbuf[zz, ab, i] = (pbuf[zz, ab, i].astype(F32) + rbuf[8 + ab * 4 + i].astype(F32)).astype(BF16)
            qcopy(ab, i).start()

    waiting = []

    def units(zz, d):
        for ab, i in ((0, m4(y + d)), (1, m4(x + d))):
            unit(zz, ab, i)
            while waiting:
                combine(*waiting.pop())
            waiting.append((zz, ab, i))

    dist = (1, -1, 2)

    def bg_copy(stage, d, incoming):
        back = d if incoming else 0
        axis = (0, 1, 2, 2, 1, 0)[stage]
        me = (y, x, zh)[axis]
        dev = (ydev, xdev, zdev)[axis](d)
        sender = m4(me - back)
        target = m4(sender + d)
        if stage < 3:
            src, dst = (s1, s2, s3)[stage].at[target], (r1, r2, r3)[stage].at[sender]
        else:
            where = [y, x, zh]
            where[axis] = sender
            src = dst = tall.at[tuple(where[: axis + 1])]
        i = stage * 3 + dist.index(d)
        return rcopy(src, dst, bs.at[i], br.at[i], dev)

    def bg_send(stage):
        for d in dist:
            c = bg_copy(stage, d, False)
            c.start()
            sent.append(c)

    def bg_recv(stage):
        for d in dist:
            bg_copy(stage, d, True).wait_recv()

    def bg_sum(stage):
        bg_recv(stage)
        if stage == 0:
            total = g32[y]
            for d in dist:
                total = total + r1[m4(y - d)].astype(F32)
            p1[...] = total
            s2[...] = total.astype(BF16)
        elif stage == 1:
            total = p1[x]
            for d in dist:
                total = total + r2[m4(x - d)].astype(F32)
            total = total.reshape(4, 16, 128)
            p2[...] = total
            s3[...] = total.astype(BF16)
        else:
            total = p2[zh]
            for d in dist:
                total = total + r3[m4(zh - d)].astype(F32)
            tall[y, x, zh] = total.astype(BF16)
        bg_send(stage + 1)

    own_away = (zh // 2 - zl) * (zh // 2 - zl)
    step = 1 - 2 * (zh % 2)
    partner, near, far = m4(zh + step), m4(zh - step), m4(zh + 2)
    p0_, p1_ = zh, own_away * partner + (1 - own_away) * near
    p2_ = own_away * near + (1 - own_away) * far
    p3_ = own_away * far + (1 - own_away) * partner
    adjacent = own_away * near + (1 - own_away) * partner

    def small_forward(zz):
        recv(zz, AXP, BYP)
        send(zz, AXFP, BYFP)
        recv(zz, AXM, BYM)
        send(zz, AXFM, BYFM)

    def big(zz):
        recv(zz, AXFP, AXFM)
        send(zz, AYP, AYM)
        recv(zz, BYFP, BYFM)
        send(zz, BXP, BXM)

    def big_forward(zz):
        recv(zz, AYP, BXP)
        send(zz, AYFP, BXFP)
        recv(zz, AYM, BXM)
        send(zz, AYFM, BXFM)

    def big_end(zz):
        recv(zz, AYFP, AYFM, BXFP, BXFM)

    for i in range(4):
        loads[i].wait()
    zsend(ZAP, ZAM, ZBP, ZBM)
    send(p0_, AXP, AXM, BYP, BYM)
    acc[...] = jnp.zeros_like(acc)
    loads[4].wait()
    norm_rows(0)
    norm_rows(1)
    small_forward(p0_)
    norm_rows(2)
    norm_rows(3)
    zrecv(ZAP, ZAM)
    zsend(ZFP)
    send(p1_, AXP, AXM)
    send(adjacent, AXP, AXM)
    norm_rows(4)
    big(p0_)
    zrecv(ZBP, ZBM)
    zsend(ZFM)
    send(p1_, BYP, BYM)
    send(adjacent, BYP, BYM)
    norm_rows(5)
    for i in range(5, first_rows):
        loads[i].wait()
    units(p0_, 0)
    small_forward(p1_)
    zrecv(ZFP, ZFM)
    send(far, AXP, AXM, BYP, BYM)
    small_forward(adjacent)
    big(p1_)
    units(p1_, 0)
    small_forward(far)
    big_forward(p0_)
    big(p2_)
    units(p2_, 0)
    block_products(0, 8)
    big_forward(p1_)
    units(p1_, 1)
    units(p1_, -1)
    big(p3_)
    block_products(8, 16)
    bg_send(0)
    big_end(p0_)
    units(p0_, 1)
    units(p0_, -1)
    big_forward(p2_)
    units(p2_, 1)
    units(p2_, -1)
    big_end(p1_)
    units(p1_, 2)
    bg_sum(0)
    units(p0_, 2)
    units(p3_, 0)
    big_forward(p3_)
    bg_sum(1)
    big_end(p2_)
    units(p2_, 2)
    bg_sum(2)
    units(p3_, 1)
    units(p3_, -1)
    bg_recv(3)
    bg_send(4)
    big_end(p3_)
    units(p3_, 2)
    combine(*waiting.pop())
    bg_recv(4)
    bg_send(5)
    key_out[...] = acc[:, 0:256].astype(BF16)
    value_out[...] = acc[:, 256:512].astype(BF16)
    for ab in range(2):
        for i in range(4):
            rwait(0, ab, i)
            n = ab * 4 + i
            rcopy(qbuf.at[n], qbuf.at[n], qs.at[n], qr.at[n], zpair).wait_recv()

    @pl.loop(0, TOK // 16)
    def _(k):
        rows = pl.ds(pl.multiple_of(k * 16, 16), 16)
        low = lanes(16)

        def tile(ab, i, half):
            cols = pl.ds(half * 128, 128)
            n = ab * 4 + i
            return pbuf[t, ab, i, rows, cols].astype(F32) + rbuf[n, rows, cols].astype(F32) + qbuf[n, rows, cols].astype(F32)

        for hx in range(2):
            for hq in range(2):
                for b in range(2):
                    a_tile = tile(0, 2 * hq + b, hx)
                    a_tiles = (a_tile, pltpu.roll(a_tile, 64, 1))
                    for a in range(2):
                        b_tile = tile(1, 2 * hx + a, hq)
                        if b == 0:
                            b_tile = pltpu.roll(b_tile, 64, 1)
                        cols = pl.ds(((2 * hx + a) * 4 + 2 * hq + b) * 128, 128)
                        grad_out[rows, cols] = jnp.where(low, a_tiles[a], b_tile).astype(BF16)

    bg_recv(5)
    bg_out[...] = tall[...].astype(F32).reshape(16, 64, 128)

    for c in sent:
        c.wait_send()
    for n in range(16):
        rcopy(pbuf.at[0, 0, 0], rbuf.at[n], ss.at[n], sr.at[n], sib).wait_send()
    for ab in range(2):
        for i in range(4):
            qcopy(ab, i).wait_send()


def local(activations, norm_gain, key_weight, value_weight, key_cot, value_cot, blocks):
    any_spec = pl.BlockSpec(memory_space=pl.ANY)
    vmem_spec = pl.BlockSpec(memory_space=pltpu.VMEM)
    dma = pltpu.SemaphoreType.DMA
    key_out, value_out, grad, bg = pl.pallas_call(
        body,
        out_shape=(
            jax.ShapeDtypeStruct((TOK, 256), BF16),
            jax.ShapeDtypeStruct((TOK, 256), BF16),
            jax.ShapeDtypeStruct((TOK, 2048), BF16),
            jax.ShapeDtypeStruct((16, 64, 128), F32),
        ),
        in_specs=[any_spec] * 6 + [pl.BlockSpec(memory_space=pltpu.SMEM)],
        out_specs=(vmem_spec,) * 4,
        scratch_shapes=[
            pltpu.VMEM((4, 4, 4, 64, 512), BF16),
            pltpu.VMEM((4, 4, 4, 64, 512), BF16),
            pltpu.VMEM((TOK, D), BF16),
            pltpu.VMEM((D // 128, TOK, 128), BF16),
            pltpu.VMEM((1, D), F32),
            pltpu.VMEM((4, TOK, 128), BF16),
            pltpu.VMEM((TOK, 512), F32),
            pltpu.VMEM((4, 2, 4, TOK, 256), BF16),
            pltpu.VMEM((16, TOK, 256), BF16),
            pltpu.VMEM((8, TOK, 256), BF16),
            pltpu.VMEM((4, 4, 64, 128), F32),
            pltpu.VMEM((4, 4, 64, 128), BF16),
            pltpu.VMEM((4, 4, 64, 128), BF16),
            pltpu.VMEM((4, 64, 128), F32),
            pltpu.VMEM((4, 64, 128), BF16),
            pltpu.VMEM((4, 64, 128), BF16),
            pltpu.VMEM((4, 16, 128), F32),
            pltpu.VMEM((4, 16, 128), BF16),
            pltpu.VMEM((4, 16, 128), BF16),
            pltpu.VMEM((4, 4, 4, 16, 128), BF16),
            dma((9 + TOK // ROWS,)),
            dma((16, 4)),
            dma((16, 4)),
            dma((6,)),
            dma((6,)),
            dma((18,)),
            dma((18,)),
            dma((16,)),
            dma((16,)),
            dma((8,)),
            dma((8,)),
        ],
        compiler_params=pltpu.CompilerParams(
            collective_id=0, has_side_effects=True, vmem_limit_bytes=60 * 1024 * 1024
        ),
        name="kv_step",
    )(
        activations,
        norm_gain.reshape(1, D),
        key_weight.reshape(4, 2, 64, 256),
        value_weight.reshape(4, 2, 64, 256),
        key_cot,
        value_cot,
        blocks.transpose(0, 2, 1),
    )
    bg = bg.reshape(16, 64, 2, 64).transpose(2, 0, 1, 3).reshape(2, 16, 4096)
    return key_out, value_out, grad, bg


def solution(mesh):
    in_specs = (
        P(("fsdp", "replica"), None),
        P(),
        P("fsdp", "tensor"),
        P("fsdp", "tensor"),
        P(("fsdp", "replica"), "tensor"),
        P(("fsdp", "replica"), "tensor"),
        P(None, "tensor", None),
    )
    out_specs = (
        P(("fsdp", "replica"), "tensor"),
        P(("fsdp", "replica"), "tensor"),
        P(("fsdp", "replica"), "tensor"),
        P(None, "tensor", None),
    )
    return jax.shard_map(local, mesh=mesh, in_specs=in_specs, out_specs=out_specs, check_vma=False)
```

time: 108 us -> 96.6 us (0.89)
  Pallas kernels: 98.3 us -> 88.7 us
  local copies, waits for them, and re-layouts: 8.39 us -> 7.02 us
    pallas_call x1, Pallas kernels: 98.3 us -> 88.7 us  [local(): pl.pallas_call(body, out_shape=(jax.ShapeDtypeStruct((TOK, 256), BF16), j...]
    unnamed x8 -> x7, local copies, waits for them, and re-layouts: 5.46 us -> 4.09 us
where the time goes in v2:
time: 96.6 us; the launch traced here: 96.4 us
  Pallas kernels  88.7 us (92%)
  local copies, waits for them, and re-layouts  7.02 us (7%)
    pallas_call x1, Pallas kernels, local(): pl.pallas_call(body, out_shape=(jax.ShapeDtypeStruct((TOK, 256), BF16), j...  88.7 us
    unnamed x7, local copies, waits for them, and re-layouts  4.09 us
    reshape x2, local copies, waits for them, and re-layouts, local(): bg = bg.reshape(16, 64, 2, 64).transpose(2, 0, 1, 3).reshape(2, 16, 4096)  2.81 us

profile of v2, /device:TPU:1, one launch (start us, length us, event | category | flops | bytes accessed | tf_op | source)
XLA Modules:
  0.0 96.4 jit_solution(17129368059018320247)
XLA Ops:
  0.6 88.7 %kv_step.1 = (bf16[384,256]{1,0:T(8,128)(2,1)}, bf16[384,256]{1,0:T(8,128)(2,1)}, bf16[384,2048]{1,0:T(8,128)(2,1)}, f32[16,64,128]{2,1,0:T(8,128)}) custom-call(bf16[384,8192]{1,0:T(8,128)(2,1)} %act_hbm.1, f32[1,8192]{1,0:T(1,128)} %bitcast.10, bf16[4,2,64,256]{3,2,1,0:T(8,128)(2,1)} %bitcast.8, bf16[4,2,64,256]{3,2,1,0:T(8,128)(2,1)} %bitcast.9, ...), custom_call_target="tpu_custom_call" | custom-call | tf_op jit(solution)/shard_map/kv_step/pallas_call | solution.py:444
  89.3 1.7 %reshape.26 = f32[16,64,2,64]{3,2,1,0:T(2,128)S(1)} reshape(f32[16,64,128]{2,1,0:T(8,128)} %get-tuple-element.11) | data formatting | bytes 1048576 | tf_op jit(solution)/shard_map/reshape | solution.py:500
  91.0 0.0 copy-start.1
  91.0 0.0 copy-start
  91.0 0.1 copy.11
  91.1 1.2 %reshape.27 = f32[2,16,4096]{2,1,0:T(8,128)} reshape(f32[2,16,64,64]{3,2,1,0:T(8,128)S(1)} %copy.11) | data formatting | bytes 1048576 | tf_op jit(solution)/shard_map/reshape | solution.py:500
  92.3 0.0 copy-done.1
  92.3 0.7 copy.15
  93.0 0.0 copy-done
  93.0 0.7 copy.16
  93.7 2.7 %copy.17 = bf16[384,2048]{1,0:T(8,128)(2,1)} copy(bf16[384,2048]{1,0:T(8,128)(2,1)} %get-tuple-element.18) | data formatting | bytes 3145728
Async XLA Ops:
  91.0 1.3 %copy-start.1 = (bf16[384,256]{1,0:T(8,128)(2,1)S(1)}, bf16[384,256]{1,0:T(8,128)(2,1)}, u32[]{:S(2)}) copy-start(bf16[384,256]{1,0:T(8,128)(2,1)} %get-tuple-element.16) | copy-start | bytes 589828
  91.0 2.0 %copy-start = (bf16[384,256]{1,0:T(8,128)(2,1)S(1)}, bf16[384,256]{1,0:T(8,128)(2,1)}, u32[]{:S(2)}) copy-start(bf16[384,256]{1,0:T(8,128)(2,1)} %get-tuple-element.17) | copy-start | bytes 589828

commit v3 on v2

--- a/solution.py
+++ b/solution.py
@@ -14,7 +14,8 @@
 BF16 = jnp.bfloat16
 ROWS = 64
 
-AXP, AXM, AXFP, AXFM, BYP, BYM, BYFP, BYFM, AYP, AYM, AYFP, AYFM, BXP, BXM, BXFP, BXFM = range(16)
+AXP, AXM, AXFP, AXFM, BYP, BYM, BYFP, BYFM = range(8)
+AYP0, AYP1, AYM0, AYM1, AYFP, AYFM, BXP0, BXP1, BXM0, BXM1, BXFP, BXFM = range(8, 20)
 ZAP, ZAM, ZBP, ZBM, ZFP, ZFM = range(6)
 
 
@@ -22,7 +23,7 @@
     act_hbm, gain_hbm, kw_hbm, vw_hbm, kc_hbm, vc_hbm, blocks,
     key_out, value_out, grad_out, bg_out,
     wa, wb, act, normed, gain, cot, acc, pbuf, rbuf, qbuf,
-    g32, s1, r1, p1, s2, r2, p2, s3, r3, tall,
+    g32, s1, r1, p1, s2, r2, p2, s3, r3, tall, gall,
     ld, xs, xr, zs, zr, bs, br, ss, sr, qs, qr,
 ):
     f = lax.axis_index("fsdp")
@@ -90,20 +91,24 @@
             return wb.at[zz, px, m4(py - 1), pl.ds(0, 32)]
         if kind == BYFM:
             return wb.at[zz, px, m4(py + 1), pl.ds(32, 32)]
-        if kind in (AYP, AYM):
-            return wa.at[zz, py]
+        if kind in (AYP0, AYM0):
+            return wa.at[zz, py, pl.ds(0, 2)]
+        if kind in (AYP1, AYM1):
+            return wa.at[zz, py, pl.ds(2, 2)]
         if kind == AYFP:
             return wa.at[zz, m4(py - 1), pl.ds(0, 2)]
         if kind == AYFM:
             return wa.at[zz, m4(py + 1), pl.ds(2, 2)]
-        if kind in (BXP, BXM):
-            return wb.at[zz, px]
+        if kind in (BXP0, BXM0):
+            return wb.at[zz, px, pl.ds(0, 2)]
+        if kind in (BXP1, BXM1):
+            return wb.at[zz, px, pl.ds(2, 2)]
         if kind == BXFP:
             return wb.at[zz, m4(px - 1), pl.ds(0, 2)]
         return wb.at[zz, m4(px + 1), pl.ds(2, 2)]
 
-    along_x = (AXP, AXM, AXFP, AXFM, BXP, BXM, BXFP, BXFM)
-    plus = (AXP, AXFP, BYP, BYFP, AYP, AYFP, BXP, BXFP)
+    along_x = (AXP, AXM, AXFP, AXFM, BXP0, BXP1, BXM0, BXM1, BXFP, BXFM)
+    plus = (AXP, AXFP, BYP, BYFP, AYP0, AYP1, AYFP, BXP0, BXP1, BXFP)
 
     def xy(kind, zz, incoming):
         d = 1 if kind in plus else -1
@@ -307,23 +312,34 @@
     p3_ = own_away * far + (1 - own_away) * partner
     adjacent = own_away * near + (1 - own_away) * partner
 
-    def small_forward(zz):
-        recv(zz, AXP, BYP)
-        send(zz, AXFP, BYFP)
-        recv(zz, AXM, BYM)
-        send(zz, AXFM, BYFM)
-
-    def big(zz):
+    def small_a(zz):
+        recv(zz, AXP)
+        send(zz, AXFP)
+        recv(zz, AXM)
+        send(zz, AXFM)
+
+    def small_b(zz):
+        recv(zz, BYP)
+        send(zz, BYFP)
+        recv(zz, BYM)
+        send(zz, BYFM)
+
+    def big_first(zz):
         recv(zz, AXFP, AXFM)
-        send(zz, AYP, AYM)
+        send(zz, AYP0, AYM1)
         recv(zz, BYFP, BYFM)
-        send(zz, BXP, BXM)
+        send(zz, BXP0, BXM1)
+
+    def big_second(zz):
+        send(zz, AYP1, AYM0, BXP1, BXM0)
 
     def big_forward(zz):
-        recv(zz, AYP, BXP)
-        send(zz, AYFP, BXFP)
-        recv(zz, AYM, BXM)
-        send(zz, AYFM, BXFM)
+        for got, kind in ((AYP0, AYFP), (BXP0, BXFP), (AYM1, AYFM), (BXM1, BXFM)):
+            recv(zz, got)
+            send(zz, kind)
+
+    def big_middle(zz):
+        recv(zz, AYP1, AYM0, BXP1, BXM0)
 
     def big_end(zz):
         recv(zz, AYFP, AYFM, BXFP, BXFM)
@@ -332,60 +348,75 @@
         loads[i].wait()
     zsend(ZAP, ZAM, ZBP, ZBM)
     send(p0_, AXP, AXM, BYP, BYM)
-    acc[...] = jnp.zeros_like(acc)
     loads[4].wait()
     norm_rows(0)
     norm_rows(1)
-    small_forward(p0_)
+    small_a(p0_)
+    small_b(p0_)
     norm_rows(2)
-    norm_rows(3)
     zrecv(ZAP, ZAM)
     zsend(ZFP)
     send(p1_, AXP, AXM)
     send(adjacent, AXP, AXM)
-    norm_rows(4)
-    big(p0_)
+    norm_rows(3)
+    big_first(p0_)
     zrecv(ZBP, ZBM)
     zsend(ZFM)
     send(p1_, BYP, BYM)
     send(adjacent, BYP, BYM)
+    big_second(p0_)
+    norm_rows(4)
     norm_rows(5)
+    small_a(p1_)
+    small_a(adjacent)
     for i in range(5, first_rows):
         loads[i].wait()
-    units(p0_, 0)
-    small_forward(p1_)
+    block_products(0, 4)
     zrecv(ZFP, ZFM)
     send(far, AXP, AXM, BYP, BYM)
-    small_forward(adjacent)
-    big(p1_)
+    big_forward(p0_)
+    block_products(4, 6)
+    small_b(p1_)
+    small_b(adjacent)
+    block_products(6, 8)
+    big_first(p1_)
+    block_products(8, 12)
+    small_a(far)
+    small_b(far)
+    big_second(p1_)
+    block_products(12, 16)
+    bg_send(0)
+    acc[...] = jnp.zeros_like(acc)
     units(p1_, 0)
-    small_forward(far)
-    big_forward(p0_)
-    big(p2_)
+    units(p0_, 0)
+    big_middle(p0_)
+    big_first(p2_)
     units(p2_, 0)
-    block_products(0, 8)
+    units(p0_, 1)
+    units(p0_, -1)
     big_forward(p1_)
+    big_middle(p1_)
+    big_second(p2_)
     units(p1_, 1)
     units(p1_, -1)
-    big(p3_)
-    block_products(8, 16)
-    bg_send(0)
+    bg_sum(0)
     big_end(p0_)
-    units(p0_, 1)
-    units(p0_, -1)
+    units(p0_, 2)
+    big_first(p3_)
+    big_end(p1_)
+    units(p1_, 2)
+    bg_sum(1)
     big_forward(p2_)
+    big_second(p3_)
+    big_middle(p2_)
     units(p2_, 1)
     units(p2_, -1)
-    big_end(p1_)
-    units(p1_, 2)
-    bg_sum(0)
-    units(p0_, 2)
-    units(p3_, 0)
     big_forward(p3_)
-    bg_sum(1)
     big_end(p2_)
     units(p2_, 2)
     bg_sum(2)
+    units(p3_, 0)
+    big_middle(p3_)
     units(p3_, 1)
     units(p3_, -1)
     bg_recv(3)
@@ -426,7 +457,15 @@
                         grad_out[rows, cols] = jnp.where(low, a_tiles[a], b_tile).astype(BF16)
 
     bg_recv(5)
-    bg_out[...] = tall[...].astype(F32).reshape(16, 64, 128)
+    gall[...] = tall[...].astype(F32).reshape(1024, 128)
+    low8 = lanes(8)
+    for h in range(2):
+        for k in range(32):
+            even = gall[pl.ds(h * 512 + 2 * k, 8, stride=64), :]
+            odd = gall[pl.ds(h * 512 + 2 * k + 1, 8, stride=64), :]
+            rows, cols = pl.ds(h * 8, 8), pl.ds(k * 128, 128)
+            bg_out[0, rows, cols] = jnp.where(low8, even, pltpu.roll(odd, 64, 1))
+            bg_out[1, rows, cols] = jnp.where(low8, pltpu.roll(even, 64, 1), odd)
 
     for c in sent:
         c.wait_send()
@@ -444,10 +483,10 @@
     key_out, value_out, grad, bg = pl.pallas_call(
         body,
         out_shape=(
-            jax.ShapeDtypeStruct((TOK, 256), BF16),
-            jax.ShapeDtypeStruct((TOK, 256), BF16),
-            jax.ShapeDtypeStruct((TOK, 2048), BF16),
-            jax.ShapeDtypeStruct((16, 64, 128), F32),
+            pltpu.VMEM((TOK, 256), BF16),
+            pltpu.VMEM((TOK, 256), BF16),
+            pltpu.VMEM((TOK, 2048), BF16),
+            pltpu.VMEM((2, 16, 4096), F32),
         ),
         in_specs=[any_spec] * 6 + [pl.BlockSpec(memory_space=pltpu.SMEM)],
         out_specs=(vmem_spec,) * 4,
@@ -472,9 +511,10 @@
             pltpu.VMEM((4, 16, 128), BF16),
             pltpu.VMEM((4, 16, 128), BF16),
             pltpu.VMEM((4, 4, 4, 16, 128), BF16),
+            pltpu.VMEM((1024, 128), F32),
             dma((9 + TOK // ROWS,)),
-            dma((16, 4)),
-            dma((16, 4)),
+            dma((20, 4)),
+            dma((20, 4)),
             dma((6,)),
             dma((6,)),
             dma((18,)),
@@ -497,7 +537,6 @@
         value_cot,
         blocks.transpose(0, 2, 1),
     )
-    bg = bg.reshape(16, 64, 2, 64).transpose(2, 0, 1, 3).reshape(2, 16, 4096)
     return key_out, value_out, grad, bg
 
 

time: 96.6 us -> 96.5 us (level); the launches traced: 96.4 us -> 94.7 us
  local copies, waits for them, and re-layouts: 7.02 us -> 3.29 us
  Pallas kernels: 88.7 us -> 90.8 us
    reshape x2 -> x0, local copies, waits for them, and re-layouts: 2.81 us -> none  [local(): bg = bg.reshape(16, 64, 2, 64).transpose(2, 0, 1, 3).reshape(2, 16, 4096)]
    pallas_call x1, Pallas kernels: 88.7 us -> 90.8 us  [local(): pl.pallas_call(body, out_shape=(pltpu.VMEM((TOK, 256), BF16), pltpu.VMEM(...]
    unnamed x7 -> x4, local copies, waits for them, and re-layouts: 4.09 us -> 3.29 us
where the time goes in v3:
time: 96.5 us; the launch traced here: 94.7 us
  Pallas kernels  90.8 us (94%)
  local copies, waits for them, and re-layouts  3.29 us (3%)
    pallas_call x1, Pallas kernels, local(): pl.pallas_call(body, out_shape=(pltpu.VMEM((TOK, 256), BF16), pltpu.VMEM(...  90.8 us
    unnamed x4, local copies, waits for them, and re-layouts  3.29 us

profile of v3, /device:TPU:1, one launch (start us, length us, event | category | flops | bytes accessed | tf_op | source)
XLA Modules:
  0.0 94.7 jit_solution(3625429549053132951)
XLA Ops:
  0.6 90.8 %kv_step.1 = (bf16[384,256]{1,0:T(8,128)(2,1)S(1)}, bf16[384,256]{1,0:T(8,128)(2,1)S(1)}, bf16[384,2048]{1,0:T(8,128)(2,1)S(1)}, f32[2,16,4096]{2,1,0:T(8,128)S(1)}) custom-call(bf16[384,8192]{1,0:T(8,128)(2,1)} %act_hbm.1, f32[1,8192]{1,0:T(1,128)} %bitcast.6, bf16[4,2,64,256]{3,2,1,0:T(8,128)(2,1)} %bitcast.4, bf16[4,2,64,256]{3,2,1,0:T(8,128)(2,1)} %bitcast.5, ...), custom_call_target="tpu_custom_call" | custom-call | tf_op jit(solution)/shard_map/kv_step/pallas_call | solution.py:483
  91.4 0.7 copy.15
  92.1 0.7 copy.16
  92.8 0.8 copy.18
  93.6 1.1 %copy.17 = bf16[384,2048]{1,0:T(8,128)(2,1)} copy(bf16[384,2048]{1,0:T(8,128)(2,1)S(1)} %get-tuple-element.6) | data formatting | bytes 3145728

commit v4 on v3

--- a/solution.py
+++ b/solution.py
@@ -23,7 +23,7 @@
     act_hbm, gain_hbm, kw_hbm, vw_hbm, kc_hbm, vc_hbm, blocks,
     key_out, value_out, grad_out, bg_out,
     wa, wb, act, normed, gain, cot, acc, pbuf, rbuf, qbuf,
-    g32, s1, r1, p1, s2, r2, p2, s3, r3, tall, gall,
+    g32, s1, r1, p1, s2, r2, gz, tall, gall,
     ld, xs, xr, zs, zr, bs, br, ss, sr, qs, qr,
 ):
     f = lax.axis_index("fsdp")
@@ -65,7 +65,7 @@
         load(act_hbm.at[pl.ds(i * ROWS, ROWS)], act.at[pl.ds(i * ROWS, ROWS)])
 
     barrier = pltpu.get_barrier_semaphore()
-    peers = [xdev(1), xdev(-1), xdev(2), ydev(1), ydev(-1), ydev(2), zdev(1), zdev(-1), zdev(2), sib, zpair]
+    peers = [xdev(1), xdev(-1), xdev(2), ydev(1), ydev(-1), ydev(2), zdev(1), zdev(-1), sib, zpair]
     for peer in peers:
         pl.semaphore_signal(barrier, inc=1, device_id=peer, device_id_type=pl.DeviceIdType.MESH)
     pl.semaphore_wait(barrier, len(peers))
@@ -258,17 +258,16 @@
 
     def bg_copy(stage, d, incoming):
         back = d if incoming else 0
-        axis = (0, 1, 2, 2, 1, 0)[stage]
-        me = (y, x, zh)[axis]
-        dev = (ydev, xdev, zdev)[axis](d)
-        sender = m4(me - back)
+        over_x = stage in (1, 2)
+        sender = m4((x if over_x else y) - back)
         target = m4(sender + d)
-        if stage < 3:
-            src, dst = (s1, s2, s3)[stage].at[target], (r1, r2, r3)[stage].at[sender]
+        dev = xdev(d) if over_x else ydev(d)
+        if stage == 0:
+            src, dst = s1.at[target], r1.at[sender]
+        elif stage == 1:
+            src, dst = s2.at[target], r2.at[sender]
         else:
-            where = [y, x, zh]
-            where[axis] = sender
-            src = dst = tall.at[tuple(where[: axis + 1])]
+            src = dst = tall.at[y, sender] if over_x else tall.at[sender]
         i = stage * 3 + dist.index(d)
         return rcopy(src, dst, bs.at[i], br.at[i], dev)
 
@@ -281,6 +280,28 @@
     def bg_recv(stage):
         for d in dist:
             bg_copy(stage, d, True).wait_recv()
+
+    turn = 2 * zl - 1
+
+    def ring(k, incoming):
+        ref = gz.at[m4(zh - (k + incoming) * turn)]
+        return rcopy(ref, ref, bs.at[12 + k], br.at[12 + k], {"fsdp": m4(zh + turn) * 4 + x})
+
+    def ring_send(k):
+        c = ring(k, 0)
+        c.start()
+        sent.append(c)
+
+    def ring_step(k):
+        ring(k, 1).wait_recv()
+        if k < 2:
+            ring_send(k + 1)
+            return
+        total = gz[0].astype(F32)
+        for i in range(1, 4):
+            total = total + gz[i].astype(F32)
+        tall[y, x] = total.astype(BF16)
+        bg_send(2)
 
     def bg_sum(stage):
         bg_recv(stage)
@@ -290,19 +311,13 @@
                 total = total + r1[m4(y - d)].astype(F32)
             p1[...] = total
             s2[...] = total.astype(BF16)
-        elif stage == 1:
+            bg_send(1)
+        else:
             total = p1[x]
             for d in dist:
                 total = total + r2[m4(x - d)].astype(F32)
-            total = total.reshape(4, 16, 128)
-            p2[...] = total
-            s3[...] = total.astype(BF16)
-        else:
-            total = p2[zh]
-            for d in dist:
-                total = total + r3[m4(zh - d)].astype(F32)
-            tall[y, x, zh] = total.astype(BF16)
-        bg_send(stage + 1)
+            gz[zh] = total.astype(BF16)
+            ring_send(0)
 
     own_away = (zh // 2 - zl) * (zh // 2 - zl)
     step = 1 - 2 * (zh % 2)
@@ -364,68 +379,67 @@
     zsend(ZFM)
     send(p1_, BYP, BYM)
     send(adjacent, BYP, BYM)
-    big_second(p0_)
     norm_rows(4)
     norm_rows(5)
-    small_a(p1_)
-    small_a(adjacent)
     for i in range(5, first_rows):
         loads[i].wait()
-    block_products(0, 4)
+    block_products(0, 5)
+    small_a(p1_)
+    small_b(p1_)
+    block_products(5, 8)
+    small_a(adjacent)
+    small_b(adjacent)
     zrecv(ZFP, ZFM)
     send(far, AXP, AXM, BYP, BYM)
-    big_forward(p0_)
-    block_products(4, 6)
-    small_b(p1_)
-    small_b(adjacent)
-    block_products(6, 8)
+    acc[...] = jnp.zeros_like(acc)
     big_first(p1_)
-    block_products(8, 12)
+    units(p1_, 0)
+    units(p0_, 0)
+    block_products(8, 11)
     small_a(far)
     small_b(far)
     big_second(p1_)
-    block_products(12, 16)
+    block_products(11, 16)
     bg_send(0)
-    acc[...] = jnp.zeros_like(acc)
-    units(p1_, 0)
-    units(p0_, 0)
-    big_middle(p0_)
     big_first(p2_)
     units(p2_, 0)
-    units(p0_, 1)
-    units(p0_, -1)
     big_forward(p1_)
+    big_second(p2_)
+    bg_sum(0)
     big_middle(p1_)
-    big_second(p2_)
     units(p1_, 1)
     units(p1_, -1)
-    bg_sum(0)
-    big_end(p0_)
-    units(p0_, 2)
-    big_first(p3_)
+    big_forward(p0_)
     big_end(p1_)
     units(p1_, 2)
     bg_sum(1)
     big_forward(p2_)
-    big_second(p3_)
+    big_second(p0_)
     big_middle(p2_)
     units(p2_, 1)
     units(p2_, -1)
-    big_forward(p3_)
+    ring_step(0)
+    big_first(p3_)
     big_end(p2_)
     units(p2_, 2)
-    bg_sum(2)
+    ring_step(1)
+    big_second(p3_)
+    big_middle(p0_)
+    big_end(p0_)
+    units(p0_, 1)
+    units(p0_, -1)
+    units(p0_, 2)
+    ring_step(2)
+    big_forward(p3_)
     units(p3_, 0)
+    bg_recv(2)
+    bg_send(3)
     big_middle(p3_)
     units(p3_, 1)
     units(p3_, -1)
-    bg_recv(3)
-    bg_send(4)
     big_end(p3_)
     units(p3_, 2)
     combine(*waiting.pop())
-    bg_recv(4)
-    bg_send(5)
     key_out[...] = acc[:, 0:256].astype(BF16)
     value_out[...] = acc[:, 256:512].astype(BF16)
     for ab in range(2):
@@ -456,7 +470,7 @@
                         cols = pl.ds(((2 * hx + a) * 4 + 2 * hq + b) * 128, 128)
                         grad_out[rows, cols] = jnp.where(low, a_tiles[a], b_tile).astype(BF16)
 
-    bg_recv(5)
+    bg_recv(3)
     gall[...] = tall[...].astype(F32).reshape(1024, 128)
     low8 = lanes(8)
     for h in range(2):
@@ -507,18 +521,16 @@
             pltpu.VMEM((4, 64, 128), F32),
             pltpu.VMEM((4, 64, 128), BF16),
             pltpu.VMEM((4, 64, 128), BF16),
-            pltpu.VMEM((4, 16, 128), F32),
-            pltpu.VMEM((4, 16, 128), BF16),
-            pltpu.VMEM((4, 16, 128), BF16),
-            pltpu.VMEM((4, 4, 4, 16, 128), BF16),
+            pltpu.VMEM((4, 64, 128), BF16),
+            pltpu.VMEM((4, 4, 64, 128), BF16),
             pltpu.VMEM((1024, 128), F32),
             dma((9 + TOK // ROWS,)),
             dma((20, 4)),
             dma((20, 4)),
             dma((6,)),
             dma((6,)),
-            dma((18,)),
-            dma((18,)),
+            dma((15,)),
+            dma((15,)),
             dma((16,)),
             dma((16,)),
             dma((8,)),

time: 96.5 us -> 82.4 us (0.85)
  the two profiles are of different devices: /device:TPU:1 before, /device:TPU:2 now
where the time goes in v4:
time: 82.4 us; the launch traced here: 82.3 us
  Pallas kernels  78.4 us (95%)
  local copies, waits for them, and re-layouts  3.29 us (4%)
    pallas_call x1, Pallas kernels, local(): pl.pallas_call(body, out_shape=(pltpu.VMEM((TOK, 256), BF16), pltpu.VMEM(...  78.4 us
    unnamed x4, local copies, waits for them, and re-layouts  3.29 us

profile of v4, /device:TPU:2, one launch (start us, length us, event | category | flops | bytes accessed | tf_op | source)
XLA Modules:
  0.0 82.3 jit_solution(16822065826334514793)
XLA Ops:
  0.6 78.4 %kv_step.1 = (bf16[384,256]{1,0:T(8,128)(2,1)S(1)}, bf16[384,256]{1,0:T(8,128)(2,1)S(1)}, bf16[384,2048]{1,0:T(8,128)(2,1)S(1)}, f32[2,16,4096]{2,1,0:T(8,128)S(1)}) custom-call(bf16[384,8192]{1,0:T(8,128)(2,1)} %act_hbm.1, f32[1,8192]{1,0:T(1,128)} %bitcast.6, bf16[4,2,64,256]{3,2,1,0:T(8,128)(2,1)} %bitcast.4, bf16[4,2,64,256]{3,2,1,0:T(8,128)(2,1)} %bitcast.5, ...), custom_call_target="tpu_custom_call" | custom-call | tf_op jit(solution)/shard_map/kv_step/pallas_call | solution.py:497
  79.0 0.7 copy.15
  79.7 0.7 copy.16
  80.4 0.8 copy.18
  81.2 1.1 %copy.17 = bf16[384,2048]{1,0:T(8,128)(2,1)} copy(bf16[384,2048]{1,0:T(8,128)(2,1)S(1)} %get-tuple-element.6) | data formatting | bytes 3145728

commit v5 on v4

--- a/solution.py
+++ b/solution.py
@@ -221,10 +221,6 @@
     def qcopy(ab, i):
         return rcopy(pbuf.at[away, ab, i], qbuf.at[ab * 4 + i], qs.at[ab * 4 + i], qr.at[ab * 4 + i], zpair)
 
-    def rwait(slot, ab, i):
-        n = slot * 8 + ab * 4 + i
-        rcopy(rbuf.at[n], rbuf.at[n], ss.at[n], sr.at[n], sib).wait_recv()
-
     def unit(zz, ab, i):
         w = (wa, wb)[ab][zz, i].reshape(256, 512)
         tile = ((ab * 4 + zz) * 4 + i) * 2
@@ -239,10 +235,14 @@
             sibcopy(zz, ab, i).start()
 
     def combine(zz, ab, i):
+        @pl.when(lax.rem(zz + t, 2) == 0)
+        def _():
+            n = sib_index(zz, ab, i)
+            rcopy(rbuf.at[n], rbuf.at[n], ss.at[n], sr.at[n], sib).wait_recv()
+            pbuf[zz, ab, i] = (pbuf[zz, ab, i].astype(F32) + rbuf[n].astype(F32)).astype(BF16)
+
         @pl.when(zz == away)
         def _():
-            rwait(1, ab, i)
-            pbuf[zz, ab, i] = (pbuf[zz, ab, i].astype(F32) + rbuf[8 + ab * 4 + i].astype(F32)).astype(BF16)
             qcopy(ab, i).start()
 
     waiting = []
@@ -442,9 +442,19 @@
     combine(*waiting.pop())
     key_out[...] = acc[:, 0:256].astype(BF16)
     value_out[...] = acc[:, 256:512].astype(BF16)
+    bg_recv(3)
+    gall[...] = tall[...].astype(F32).reshape(1024, 128)
+    low8 = lanes(8)
+    for h in range(2):
+        for k in range(32):
+            even = gall[pl.ds(h * 512 + 2 * k, 8, stride=64), :]
+            odd = gall[pl.ds(h * 512 + 2 * k + 1, 8, stride=64), :]
+            rows, cols = pl.ds(h * 8, 8), pl.ds(k * 128, 128)
+            bg_out[0, rows, cols] = jnp.where(low8, even, pltpu.roll(odd, 64, 1))
+            bg_out[1, rows, cols] = jnp.where(low8, pltpu.roll(even, 64, 1), odd)
+
     for ab in range(2):
         for i in range(4):
-            rwait(0, ab, i)
             n = ab * 4 + i
             rcopy(qbuf.at[n], qbuf.at[n], qs.at[n], qr.at[n], zpair).wait_recv()
 
@@ -456,7 +466,7 @@
         def tile(ab, i, half):
             cols = pl.ds(half * 128, 128)
             n = ab * 4 + i
-            return pbuf[t, ab, i, rows, cols].astype(F32) + rbuf[n, rows, cols].astype(F32) + qbuf[n, rows, cols].astype(F32)
+            return pbuf[t, ab, i, rows, cols].astype(F32) + qbuf[n, rows, cols].astype(F32)
 
         for hx in range(2):
             for hq in range(2):
@@ -470,17 +480,6 @@
                         cols = pl.ds(((2 * hx + a) * 4 + 2 * hq + b) * 128, 128)
                         grad_out[rows, cols] = jnp.where(low, a_tiles[a], b_tile).astype(BF16)
 
-    bg_recv(3)
-    gall[...] = tall[...].astype(F32).reshape(1024, 128)
-    low8 = lanes(8)
-    for h in range(2):
-        for k in range(32):
-            even = gall[pl.ds(h * 512 + 2 * k, 8, stride=64), :]
-            odd = gall[pl.ds(h * 512 + 2 * k + 1, 8, stride=64), :]
-            rows, cols = pl.ds(h * 8, 8), pl.ds(k * 128, 128)
-            bg_out[0, rows, cols] = jnp.where(low8, even, pltpu.roll(odd, 64, 1))
-            bg_out[1, rows, cols] = jnp.where(low8, pltpu.roll(even, 64, 1), odd)
-
     for c in sent:
         c.wait_send()
     for n in range(16):
@@ -488,6 +487,14 @@
     for ab in range(2):
         for i in range(4):
             qcopy(ab, i).wait_send()
+
+
+def write_out(*refs):
+    copies = [pltpu.make_async_copy(refs[i], refs[4 + i], refs[8].at[i]) for i in range(4)]
+    for c in copies:
+        c.start()
+    for c in copies:
+        c.wait()
 
 
 def local(activations, norm_gain, key_weight, value_weight, key_cot, value_cot, blocks):
@@ -549,7 +556,16 @@
         value_cot,
         blocks.transpose(0, 2, 1),
     )
-    return key_out, value_out, grad, bg
+    results = (key_out, value_out, grad, bg)
+    return pl.pallas_call(
+        write_out,
+        out_shape=tuple(jax.ShapeDtypeStruct(r.shape, r.dtype) for r in results),
+        in_specs=[any_spec] * 4,
+        out_specs=(any_spec,) * 4,
+        scratch_shapes=[dma((4,))],
+        compiler_params=pltpu.CompilerParams(vmem_limit_bytes=1024 * 1024),
+        name="write_out",
+    )(*results)
 
 
 def solution(mesh):

time: 82.4 us -> 80.2 us (0.973)
  local copies, waits for them, and re-layouts: 3.29 us -> 0 us
  Pallas kernels: 78.4 us -> 79.3 us
    unnamed x4 -> x0, local copies, waits for them, and re-layouts: 3.29 us -> none
    pallas_call x0 -> x1, Pallas kernels: none -> 1.48 us  [local(): pl.pallas_call(write_out, out_shape=tuple((jax.ShapeDtypeStruct(r.shape,...]
where the time goes in v5:
time: 80.2 us; the launch traced here: 80.1 us
  Pallas kernels  79.3 us (99%)
    pallas_call x1, Pallas kernels, local(): pl.pallas_call(body, out_shape=(pltpu.VMEM((TOK, 256), BF16), pltpu.VMEM(...  77.8 us

profile of v5, /device:TPU:2, one launch (start us, length us, event | category | flops | bytes accessed | tf_op | source)
XLA Modules:
  0.0 80.1 jit_solution(3094650715624854467)
XLA Ops:
  0.6 77.8 %kv_step.1 = (bf16[384,256]{1,0:T(8,128)(2,1)S(1)}, bf16[384,256]{1,0:T(8,128)(2,1)S(1)}, bf16[384,2048]{1,0:T(8,128)(2,1)S(1)}, f32[2,16,4096]{2,1,0:T(8,128)S(1)}) custom-call(bf16[384,8192]{1,0:T(8,128)(2,1)} %act_hbm.1, f32[1,8192]{1,0:T(1,128)} %bitcast.6, bf16[4,2,64,256]{3,2,1,0:T(8,128)(2,1)} %bitcast.4, bf16[4,2,64,256]{3,2,1,0:T(8,128)(2,1)} %bitcast.5, ...), custom_call_target="tpu_custom_call" | custom-call | tf_op jit(solution)/shard_map/kv_step/pallas_call | solution.py:504
  78.4 1.5 %write_out.1 = (bf16[384,256]{1,0:T(8,128)(2,1)}, bf16[384,256]{1,0:T(8,128)(2,1)}, bf16[384,2048]{1,0:T(8,128)(2,1)}, f32[2,16,4096]{2,1,0:T(8,128)}) custom-call(bf16[384,256]{1,0:T(8,128)(2,1)S(1)} %get-tuple-element.8.refs_0_, bf16[384,256]{1,0:T(8,128)(2,1)S(1)} %get-tuple-element.9.refs_1_, bf16[384,2048]{1,0:T(8,128)(2,1)S(1)} %get-tuple-element.10.refs_2_, ...), custom_call_target="tpu_custom_call" | custom-call | tf_op jit(solution)/shard_map/write_out/pallas_call | solution.py:560

commit v6 on v5

--- a/solution.py
+++ b/solution.py
@@ -410,28 +410,28 @@
     units(p1_, 1)
     units(p1_, -1)
     big_forward(p0_)
+    big_second(p0_)
     big_end(p1_)
     units(p1_, 2)
+    big_forward(p2_)
+    big_first(p3_)
     bg_sum(1)
-    big_forward(p2_)
-    big_second(p0_)
     big_middle(p2_)
     units(p2_, 1)
     units(p2_, -1)
+    big_middle(p0_)
+    units(p0_, 1)
+    units(p0_, -1)
     ring_step(0)
-    big_first(p3_)
+    big_second(p3_)
+    big_end(p0_)
+    units(p0_, 2)
+    ring_step(1)
     big_end(p2_)
     units(p2_, 2)
-    ring_step(1)
-    big_second(p3_)
-    big_middle(p0_)
-    big_end(p0_)
-    units(p0_, 1)
-    units(p0_, -1)
-    units(p0_, 2)
-    ring_step(2)
     big_forward(p3_)
     units(p3_, 0)
+    ring_step(2)
     bg_recv(2)
     bg_send(3)
     big_middle(p3_)

time: 80.2 us -> 80.1 us (level)
  the two profiles are of different devices: /device:TPU:2 before, /device:TPU:1 now
where the time goes in v6:
time: 80.1 us; the launch traced here: 80 us
  Pallas kernels  79.2 us (99%)
    pallas_call x1, Pallas kernels, local(): pl.pallas_call(body, out_shape=(pltpu.VMEM((TOK, 256), BF16), pltpu.VMEM(...  77.7 us

profile of v6, /device:TPU:1, one launch (start us, length us, event | category | flops | bytes accessed | tf_op | source)
XLA Modules:
  0.0 80.0 jit_solution(17025249747683900356)
XLA Ops:
  0.6 77.7 %kv_step.1 = (bf16[384,256]{1,0:T(8,128)(2,1)S(1)}, bf16[384,256]{1,0:T(8,128)(2,1)S(1)}, bf16[384,2048]{1,0:T(8,128)(2,1)S(1)}, f32[2,16,4096]{2,1,0:T(8,128)S(1)}) custom-call(bf16[384,8192]{1,0:T(8,128)(2,1)} %act_hbm.1, f32[1,8192]{1,0:T(1,128)} %bitcast.6, bf16[4,2,64,256]{3,2,1,0:T(8,128)(2,1)} %bitcast.4, bf16[4,2,64,256]{3,2,1,0:T(8,128)(2,1)} %bitcast.5, ...), custom_call_target="tpu_custom_call" | custom-call | tf_op jit(solution)/shard_map/kv_step/pallas_call | solution.py:504
  78.4 1.5 %write_out.1 = (bf16[384,256]{1,0:T(8,128)(2,1)}, bf16[384,256]{1,0:T(8,128)(2,1)}, bf16[384,2048]{1,0:T(8,128)(2,1)}, f32[2,16,4096]{2,1,0:T(8,128)}) custom-call(bf16[384,256]{1,0:T(8,128)(2,1)S(1)} %get-tuple-element.8.refs_0_, bf16[384,256]{1,0:T(8,128)(2,1)S(1)} %get-tuple-element.9.refs_1_, bf16[384,2048]{1,0:T(8,128)(2,1)S(1)} %get-tuple-element.10.refs_2_, ...), custom_call_target="tpu_custom_call" | custom-call | tf_op jit(solution)/shard_map/write_out/pallas_call | solution.py:560

commit v7 on v6

--- a/solution.py
+++ b/solution.py
@@ -258,7 +258,7 @@
 
     def bg_copy(stage, d, incoming):
         back = d if incoming else 0
-        over_x = stage in (1, 2)
+        over_x = stage in (1, 3)
         sender = m4((x if over_x else y) - back)
         target = m4(sender + d)
         dev = xdev(d) if over_x else ydev(d)
@@ -267,7 +267,7 @@
         elif stage == 1:
             src, dst = s2.at[target], r2.at[sender]
         else:
-            src = dst = tall.at[y, sender] if over_x else tall.at[sender]
+            src = dst = tall.at[sender] if over_x else tall.at[x, sender]
         i = stage * 3 + dist.index(d)
         return rcopy(src, dst, bs.at[i], br.at[i], dev)
 
@@ -300,7 +300,7 @@
         total = gz[0].astype(F32)
         for i in range(1, 4):
             total = total + gz[i].astype(F32)
-        tall[y, x] = total.astype(BF16)
+        tall[x, y] = total.astype(BF16)
         bg_send(2)
 
     def bg_sum(stage):
@@ -443,7 +443,8 @@
     key_out[...] = acc[:, 0:256].astype(BF16)
     value_out[...] = acc[:, 256:512].astype(BF16)
     bg_recv(3)
-    gall[...] = tall[...].astype(F32).reshape(1024, 128)
+    for i in range(16):
+        gall[pl.ds(i * 64, 64), :] = tall[i % 4, i // 4].astype(F32)
     low8 = lanes(8)
     for h in range(2):
         for k in range(32):

time: 80.1 us -> 80.1 us (level)
  no operation moved by 1% of the time
where the time goes in v7:
time: 80.1 us; the launch traced here: 80 us
  Pallas kernels  79.2 us (99%)
    pallas_call x1, Pallas kernels, local(): pl.pallas_call(body, out_shape=(pltpu.VMEM((TOK, 256), BF16), pltpu.VMEM(...  77.7 us

profile of v7, /device:TPU:1, one launch (start us, length us, event | category | flops | bytes accessed | tf_op | source)
XLA Modules:
  0.0 80.0 jit_solution(1009002270729970997)
XLA Ops:
  0.6 77.7 %kv_step.1 = (bf16[384,256]{1,0:T(8,128)(2,1)S(1)}, bf16[384,256]{1,0:T(8,128)(2,1)S(1)}, bf16[384,2048]{1,0:T(8,128)(2,1)S(1)}, f32[2,16,4096]{2,1,0:T(8,128)S(1)}) custom-call(bf16[384,8192]{1,0:T(8,128)(2,1)} %act_hbm.1, f32[1,8192]{1,0:T(1,128)} %bitcast.6, bf16[4,2,64,256]{3,2,1,0:T(8,128)(2,1)} %bitcast.4, bf16[4,2,64,256]{3,2,1,0:T(8,128)(2,1)} %bitcast.5, ...), custom_call_target="tpu_custom_call" | custom-call | tf_op jit(solution)/shard_map/kv_step/pallas_call | solution.py:505
  78.4 1.5 %write_out.1 = (bf16[384,256]{1,0:T(8,128)(2,1)}, bf16[384,256]{1,0:T(8,128)(2,1)}, bf16[384,2048]{1,0:T(8,128)(2,1)}, f32[2,16,4096]{2,1,0:T(8,128)}) custom-call(bf16[384,256]{1,0:T(8,128)(2,1)S(1)} %get-tuple-element.8.refs_0_, bf16[384,256]{1,0:T(8,128)(2,1)S(1)} %get-tuple-element.9.refs_1_, bf16[384,2048]{1,0:T(8,128)(2,1)S(1)} %get-tuple-element.10.refs_2_, ...), custom_call_target="tpu_custom_call" | custom-call | tf_op jit(solution)/shard_map/write_out/pallas_call | solution.py:561
